TPU v7x, 32 devices: a whole 2x2x4 slice. The times are simulated.
32 devices in a mesh: section: 2 (over x), patch: 4 (over z), fsdp: 4 (over y, core).
Axes of the slice: x: 2, y: 2, z: 4, core: 2. Of those that a mesh axis runs over, the one named last changes fastest.
Arguments:
- latent: float32 [8, 4, 256, 64], P('fsdp', 'patch', 'section'), may hold values from -60 to 60
- counts: int32 [8, 4], P('fsdp'), may hold values from 64 to 256, as said below
- steps_idx: int32 [8], P('fsdp'), may hold values from 0 to 49
- embed_weight: bfloat16 [64, 1536], replicated, may hold values from -0.75 to 0.75
- wqkv: bfloat16 [2, 1536, 4608], P('section', 'fsdp'), may hold values from -0.15625 to 0.15625
- wo: bfloat16 [2, 1536, 1536], P('section', 'fsdp'), may hold values from -0.15625 to 0.15625
- qk_gain: float32 [2, 3072], P('section'), may hold values from 0.1 to 1.9
- modulation: float32 [2, 50, 4608], P('section'), may hold values from -3 to 3
- head_mod: float32 [50, 3072], replicated, may hold values from -3 to 3
- head_weight: bfloat16 [1536, 64], replicated, may hold values from -0.15625 to 0.15625
- stale_cache: bfloat16 [2, 8, 4, 256, 3072], P('section', 'fsdp', 'patch'), may hold values from -210 to 210
Outputs:
- velocity: float32 [8, 4, 256, 64], P('fsdp', 'patch', 'section')
- new_latent: float32 [8, 4, 256, 64], P('fsdp', 'patch', 'section')
- cache_out: bfloat16 [2, 8, 4, 256, 3072], P('section', 'fsdp', 'patch')
Inputs may be any that keep to these rules, and one draw needn't show every extreme that they name: `counts`: in every video one patch holds exactly 256 tokens.
All inputs are finite; a program needn't handle non-finite values.
Results may differ from a plain program's by a relative error of at most 0.0071.
Values may be sent and summed in bfloat16 or wider, within the bound.
A program may use at most 192 MiB of HBM per device.

v0:
```python
import math
import jax
import jax.numpy as jnp
from jax import lax
from jax.sharding import PartitionSpec as P

HEADS = 12
HD = 128
TSTEPS = 50
EPS = 1e-06


def shifted(shard, axis, by):
    devices = lax.axis_size(axis)
    pairs = [(i, i + by) for i in range(devices) if 0 <= i + by < devices]
    return lax.ppermute(shard, axis, pairs)


def layer_norm(hidden):
    center = hidden - jnp.mean(hidden, axis=-1, keepdims=True)
    return center * lax.rsqrt(jnp.mean(center * center, axis=-1, keepdims=True) + EPS)


def rms_norm(values_in, gain_vec):
    return (
        values_in
        * lax.rsqrt(jnp.mean(values_in * values_in, axis=-1, keepdims=True) + EPS)
        * gain_vec
    )


def sigma_of(step_float):
    remain = 1.0 - step_float / TSTEPS
    return 5.0 * remain / (1.0 + 4.0 * remain)


def dense_attend(queries, key_rows, value_rows, key_live):
    groups, query_count = (queries.shape[0], queries.shape[1])
    query_heads = queries.reshape(groups, query_count, HEADS, HD)
    key_heads = key_rows.reshape(groups, key_rows.shape[1], HEADS, HD)
    value_heads = value_rows.reshape(groups, value_rows.shape[1], HEADS, HD)
    scores = jnp.einsum(
        "gqhd,gkhd->ghqk", query_heads, key_heads, preferred_element_type=jnp.float32
    ) / math.sqrt(HD)
    scores = jnp.where(key_live[:, None, None, :], scores, -jnp.inf)
    top_score = jnp.max(scores, axis=-1, keepdims=True)
    exp_scores = jnp.exp(scores - top_score)
    denom_sum = jnp.sum(exp_scores, axis=-1)
    mixed_out = jnp.einsum(
        "ghqk,gkhd->gqhd",
        exp_scores.astype(jnp.bfloat16),
        value_heads,
        preferred_element_type=jnp.float32,
    )
    mixed_out = mixed_out / jnp.transpose(denom_sum, (0, 2, 1))[..., None]
    return mixed_out.reshape(groups, query_count, HEADS * HD).astype(jnp.bfloat16)


def run_layer(hidden, modulation_rows, project_in, project_out, gain_rows, attend_fn):
    groups, slot_count, model_width = hidden.shape
    shift_vec = modulation_rows[:, None, :model_width]
    scale_vec = modulation_rows[:, None, model_width : 2 * model_width]
    gate_vec = modulation_rows[:, None, 2 * model_width :]
    normed = (layer_norm(hidden) * (1.0 + scale_vec) + shift_vec).astype(jnp.bfloat16)
    projected = project_in(normed.reshape(-1, model_width))
    projected = projected.reshape(groups, slot_count, 3 * model_width)
    queries = rms_norm(projected[..., :model_width], gain_rows[:model_width]).astype(jnp.bfloat16)
    fresh_keys = rms_norm(
        projected[..., model_width : 2 * model_width], gain_rows[model_width:]
    ).astype(jnp.bfloat16)
    fresh_values = projected[..., 2 * model_width :].astype(jnp.bfloat16)
    fresh_kv = jnp.concatenate([fresh_keys, fresh_values], axis=-1)
    attended = attend_fn(queries, fresh_kv)
    update = project_out(attended.reshape(-1, model_width))
    return (hidden + gate_vec * update.reshape(groups, slot_count, model_width), fresh_kv)


def body(
    latent,
    counts,
    steps_idx,
    embed_weight,
    wqkv,
    wo,
    qk_gain,
    modulation,
    head_mod,
    head_weight,
    stale_cache,
):
    section_index = lax.axis_index("section")
    own_patch = lax.axis_index("patch")
    first_section = section_index == 0
    videos = latent.shape[0]
    patch_rows = stale_cache.shape[3]
    model_width = embed_weight.shape[1]
    patch_count = counts.shape[1]
    zero_index = jnp.zeros((), jnp.int32)
    proj_full, out_full = (
        lax.all_gather(wqkv, "fsdp", axis=1, tiled=True),
        lax.all_gather(wo, "fsdp", axis=1, tiled=True),
    )
    proj_full = proj_full[0]
    out_full = out_full[0]

    def project_in(left):
        return jnp.dot(left, proj_full, preferred_element_type=jnp.float32)

    def project_out(left):
        return jnp.dot(left, out_full, preferred_element_type=jnp.float32)

    rows_full = lax.all_gather(latent.astype(jnp.bfloat16), "section", axis=2, tiled=True)
    start_hidden = jnp.dot(
        rows_full.reshape(-1, rows_full.shape[3]), embed_weight, preferred_element_type=jnp.float32
    )
    start_hidden = start_hidden.reshape(videos, patch_rows, model_width)
    step_onehot = (jnp.arange(TSTEPS, dtype=jnp.int32)[None, :] == steps_idx[:, None]).astype(
        jnp.float32
    )
    modulation_all = jnp.dot(step_onehot, modulation[0], precision=lax.Precision.HIGHEST)
    head_rows = jnp.dot(step_onehot, head_mod, precision=lax.Precision.HIGHEST)
    gain_rows = qk_gain[0]
    slot_iota = jnp.arange(patch_rows, dtype=jnp.int32)
    own_count = jnp.sum(
        jnp.where(jnp.arange(patch_count, dtype=jnp.int32)[None, :] == own_patch, counts, 0), axis=1
    )
    own_live = slot_iota[None, :] < own_count[:, None]
    key_live_all = (slot_iota[None, None, :] < counts[:, :, None]).reshape(
        videos, patch_count * patch_rows
    )
    stale_all = lax.all_gather(stale_cache, "patch", axis=2, tiled=True)[0].reshape(
        videos, patch_count * patch_rows, 2 * model_width
    )
    group_size = videos // videos
    received = jnp.zeros((group_size, patch_rows, model_width), jnp.float32)
    hidden_end = jnp.zeros((videos, patch_rows, model_width), jnp.float32)
    cache_buf = jnp.zeros((videos, patch_rows, 2 * model_width), jnp.bfloat16)
    for tick_index in range(videos + 1):
        group_index = jnp.clip(
            jnp.where(first_section, tick_index, tick_index - 1), 0, videos - 1
        ).astype(jnp.int32)
        first_video = group_index * group_size
        source_group = min(tick_index, videos - 1)
        source_zero = start_hidden[source_group * group_size : (source_group + 1) * group_size]
        hidden_in = jnp.where(first_section, source_zero, received)
        modulation_group = lax.dynamic_slice_in_dim(modulation_all, first_video, group_size, 0)
        stale_group = lax.dynamic_slice_in_dim(stale_all, first_video, group_size, 0)
        live_group = lax.dynamic_slice_in_dim(key_live_all, first_video, group_size, 0)

        def attend_fn(queries, fresh_kv, stale_group=stale_group, live_group=live_group):
            seen_rows = lax.dynamic_update_slice(
                stale_group, fresh_kv, (zero_index, own_patch * patch_rows, zero_index)
            )
            return dense_attend(
                queries, seen_rows[..., :model_width], seen_rows[..., model_width:], live_group
            )

        hidden_out, fresh_kv = run_layer(
            hidden_in, modulation_group, project_in, project_out, gain_rows, attend_fn
        )
        own_group = lax.dynamic_slice_in_dim(own_live, first_video, group_size, 0)
        fresh_kv = jnp.where(own_group[..., None], fresh_kv, jnp.zeros_like(fresh_kv))
        is_valid = jnp.where(first_section, tick_index < videos, tick_index >= 1)
        cache_buf = jnp.where(
            is_valid,
            lax.dynamic_update_slice(cache_buf, fresh_kv, (first_video, zero_index, zero_index)),
            cache_buf,
        )
        hidden_end = jnp.where(
            is_valid,
            lax.dynamic_update_slice(hidden_end, hidden_out, (first_video, zero_index, zero_index)),
            hidden_end,
        )
        if tick_index < videos:
            received = shifted(hidden_out.astype(jnp.bfloat16), "section", 1).astype(jnp.float32)
    head_in = (
        layer_norm(hidden_end) * (1.0 + head_rows[:, None, model_width:])
        + head_rows[:, None, :model_width]
    ).astype(jnp.bfloat16)
    velocity = jnp.dot(
        head_in.reshape(-1, model_width), head_weight, preferred_element_type=jnp.float32
    )
    velocity = velocity.reshape(videos, patch_rows, head_weight.shape[1])
    velocity = jnp.where(own_live[..., None], velocity, jnp.zeros_like(velocity))
    half_rows = patch_rows // 2
    returned = shifted(velocity[:, :half_rows].astype(jnp.bfloat16), "section", -1).astype(
        jnp.float32
    )
    mine_half = jnp.where(first_section, returned, velocity[:, half_rows:])
    step_float = steps_idx.astype(jnp.float32)
    step_delta = sigma_of(step_float + 1.0) - sigma_of(step_float)
    new_latent = latent + step_delta[:, None, None, None] * mine_half[:, None]
    return (mine_half[:, None], new_latent, cache_buf[None, :, None])


def solution(mesh):
    in_specs = (
        P("fsdp", "patch", "section", None),
        P("fsdp", None),
        P("fsdp"),
        P(),
        P("section", "fsdp", None),
        P("section", "fsdp", None),
        P("section", None),
        P("section", None, None),
        P(),
        P(),
        P("section", "fsdp", "patch", None, None),
    )
    out_specs = (
        P("fsdp", "patch", "section", None),
        P("fsdp", "patch", "section", None),
        P("section", "fsdp", "patch", None, None),
    )
    return jax.shard_map(body, mesh=mesh, in_specs=in_specs, out_specs=out_specs, check_vma=False)
```

profile of v0, /device:TPU:0, one launch (start us, length us, event | category | flops | bytes accessed | tf_op | source)
XLA Modules:
  0.0 515.3 jit_solution(11341558818491198296)
XLA Ops:
  9.5 5.5 %all_gather.12 = bf16[2,1,256,64]{2,3,1,0:T(8,128)(2,1)S(1)} all-gather(bf16[2,1,128,64]{2,3,1,0:T(8,128)(2,1)S(1)} %convert_element_type.99), channel_id=1, replica_groups=mesh['section'=2,'patch'=4,'fsdp'=4] {'section'}, dimensions={2}, use_global_device_ids=true | all-gather | bytes 98304 | tf_op jit(solution)/shard_map/all_gather | solution.py:112
  18.8 211.8 %all-gather.4.cloned.1.call-done = bf16[1,2,4,256,3072]{4,3,2,1,0:T(8,128)(2,1)} async-done(((bf16[1,2,1,256,3072]{4,3,2,1,0:T(8,128)(2,1)}), bf16[1,2,4,256,3072]{4,3,2,1,0:T(8,128)(2,1)}) %all-gather.4.cloned.1.call-update) | async-done | bytes 12582928 | tf_op jit(solution)/shard_map/all_gather | solution.py:131
  230.6 16.0 %constant_dynamic-slice_fusion.3 = (bf16[1,1024,3072]{2,1,0:T(8,128)(2,1)}, bf16[1,1024,3072]{2,1,0:T(8,128)(2,1)}, bf16[1,1024,3072]{2,1,0:T(8,128)(2,1)}) fusion(bf16[2,1024,3072]{2,1,0:T(8,128)(2,1)} %bitcast.193, s32[]{:T(128)S(6)} %min.12, s32[]{:T(128)S(6)} %min.11, s32[]{:T(128)S(6)} %min.10), kind=kLoop, calls=%fused_computation.146 | loop fusion | bytes 37748748 | tf_op jit(solution)/shard_map/dynamic_slice | solution.py:147
  246.6 8.7 %copy.54 = bf16[1,1024,3072]{1,2,0:T(8,128)(2,1)} copy(bf16[1,1024,3072]{2,1,0:T(8,128)(2,1)} %get-tuple-element.34) | data formatting | bytes 12582912
  255.3 66.1 %all-gather.6.cloned.1.call-done = bf16[1,1536,4608]{2,1,0:T(8,128)(2,1)} async-done(((bf16[1,384,4608]{2,1,0:T(8,128)(2,1)}), bf16[1,1536,4608]{2,1,0:T(8,128)(2,1)}) %all-gather.6.cloned.1.call-update) | async-done | bytes 14155792 | tf_op jit(solution)/shard_map/all_gather | solution.py:100
  321.4 7.8 %fusion.15 = f32[1,256,4608]{2,1,0:T(8,128)S(1)} fusion(bf16[1,1536,4608]{2,1,0:T(8,128)(2,1)} %all-gather.6.cloned.1.call-done, f32[512,1536]{1,0:T(8,128)} %copy-done.1, f32[1536]{0:T(1024)S(1)} %get-tuple-element.23, f32[1536]{0:T(1024)S(1)} %get-tuple-element.19, f32[256]{0:T(256)S(1)} %add_rsqrt_fusion.9, f32[256]{0:T(256)S(1)} %broadcast_multiply_fusion.3, ...), kind=kOutput, calls=%fused_computation.21 | convolution fusion | flops 3626237952 | bytes 20461568 | tf_op jit(solution)/shard_map/dot_general | solution.py:107
  329.9 2.1 broadcast_in_dim.155
  332.0 1.8 select_dynamic-update-slice_fusion.1
  335.6 2.7 constant_dynamic-update-slice_fusion.3
  338.3 3.6 fusion.134
  341.9 2.0 fusion.6
  343.9 3.0 fusion.9
  347.0 3.3 fusion.80
  350.3 10.2 %all-gather.8.cloned.1.call-done = bf16[1,1536,1536]{2,1,0:T(8,128)(2,1)} async-done(((bf16[1,384,1536]{2,1,0:T(8,128)(2,1)}), bf16[1,1536,1536]{2,1,0:T(8,128)(2,1)}) %all-gather.8.cloned.1.call-update) | async-done | bytes 4718608 | tf_op jit(solution)/shard_map/all_gather | solution.py:101
  360.5 2.0 broadcast_in_dim.85
  363.5 4.9 bitcast_dynamic-update-slice_fusion.1
  368.4 3.4 collective-permute-start
  371.8 8.8 %copy.55 = bf16[1,1024,3072]{1,2,0:T(8,128)(2,1)} copy(bf16[1,1024,3072]{2,1,0:T(8,128)(2,1)} %get-tuple-element.33) | data formatting | bytes 12582912
  380.6 8.3 %collective-permute-done = bf16[1,256,1536]{2,1,0:T(8,128)(2,1)S(1)} collective-permute-done((bf16[1,256,1536]{2,1,0:T(8,128)(2,1)S(1)}, bf16[1,256,1536]{2,1,0:T(8,128)(2,1)S(1)}, u32[]{:S(2)}, u32[]{:S(2)}) %collective-permute-start) | collective-permute-done | bytes 786464 | tf_op jit(solution)/shard_map/ppermute | solution.py:16
  389.0 1.6 fusion.130
  390.6 1.8 multiply_reduce_fusion.6
  392.4 7.5 %fusion.18 = f32[1,256,4608]{2,1,0:T(8,128)S(1)} fusion(bf16[1,1536,4608]{2,1,0:T(8,128)(2,1)} %all-gather.6.cloned.1.call-done, f32[1536]{0:T(1024)S(1)} %get-tuple-element.22, f32[1536]{0:T(1024)S(1)} %get-tuple-element.17, f32[256]{0:T(256)S(1)} %add_rsqrt_fusion.6, f32[256]{0:T(256)S(1)} %broadcast_multiply_fusion.2, ...), kind=kOutput, calls=%fused_computation.22 | convolution fusion | flops 3626631168 | bytes 21252096 | tf_op jit(solution)/shard_map/dot_general | solution.py:107
  401.5 1.8 select_dynamic-update-slice_fusion
  403.3 1.6 copy.33
  404.9 2.7 constant_dynamic-update-slice_fusion.2
  407.6 6.3 %fusion.133 = (bf16[1,1024,1536]{1,2,0:T(8,128)(2,1)}, bf16[1,1024,1536]{1,2,0:T(8,128)(2,1)}) fusion(bf16[1,1024,3072]{1,2,0:T(8,128)(2,1)} %constant_dynamic-update-slice_fusion.2), kind=kLoop, calls=%fused_computation.190 | loop fusion | bytes 12582912 | tf_op jit(solution)/shard_map/slice | solution.py:155
  414.2 3.9 fusion.7
  418.1 3.0 fusion.11
  421.2 4.7 fusion.79
  425.9 4.9 fusion.135
  430.9 4.4 collective-permute-start.1
  435.6 8.8 %copy.56 = bf16[1,1024,3072]{1,2,0:T(8,128)(2,1)} copy(bf16[1,1024,3072]{2,1,0:T(8,128)(2,1)} %get-tuple-element.32) | data formatting | bytes 12582912
  444.5 3.9 copy.72
  448.4 3.2 collective-permute-done.1
  452.2 7.5 %fusion.21 = f32[1,256,4608]{2,1,0:T(8,128)S(1)} fusion(bf16[1,1536,4608]{2,1,0:T(8,128)(2,1)} %all-gather.6.cloned.1.call-done, f32[1536]{0:T(1024)S(1)} %get-tuple-element.21, f32[1536]{0:T(1024)S(1)} %get-tuple-element.16, f32[256]{0:T(256)S(1)} %add_rsqrt_fusion.3, f32[256]{0:T(256)S(1)} %broadcast_multiply_fusion.1, ...), kind=kOutput, calls=%fused_computation.23 | convolution fusion | flops 3626631168 | bytes 21252096 | tf_op jit(solution)/shard_map/dot_general | solution.py:107
  462.6 2.6 copy.37
  465.2 2.7 constant_dynamic-update-slice_fusion
  467.9 6.2 %fusion.132 = (bf16[1,1024,1536]{1,2,0:T(8,128)(2,1)}, bf16[1,1024,1536]{1,2,0:T(8,128)(2,1)}) fusion(bf16[1,1024,3072]{1,2,0:T(8,128)(2,1)} %constant_dynamic-update-slice_fusion), kind=kLoop, calls=%fused_computation.189 | loop fusion | bytes 12582912 | tf_op jit(solution)/shard_map/slice | solution.py:155
  474.1 2.3 copy.38
  476.4 4.2 fusion.8
  480.6 3.0 fusion.13
  483.6 4.7 fusion.78
  488.4 5.5 %fusion.72 = f32[2,256,1536]{2,1,0:T(8,128)} fusion(f32[2,256,1536]{2,1,0:T(8,128)} %get-tuple-element.52, s32[]{:T(128)S(6)} %min.12, bf16[256,1536]{0,1:T(8,128)(2,1)S(1)} %bitcast.204, bf16[1,1536,1536]{2,1,0:T(8,128)(2,1)} %all-gather.8.cloned.1.call-done, f32[1536]{0:T(1024)S(1)} %get-tuple-element.15, pred[]{:T(512)S(6)} %select_n.179, ...), kind=kOutput, calls=%fused_computation.55 | convolution fusion | flops 1209925632 | bytes 11016198 | tf_op jit(solution)/shard_map/dot_general | solution.py:110
  493.9 2.2 reduce_sum.187
  496.0 2.5 multiply_reduce_fusion
  498.6 2.7 fusion.88
  502.6 2.3 bitcast_dynamic-update-slice_fusion
  504.9 2.2 collective-permute-done.2
  (94 shorter events, 17.8 us)
Async XLA Ops:
  7.2 428.1 %copy-start = (f32[50,3072]{1,0:T(8,128)S(1)}, f32[50,3072]{1,0:T(8,128)}, u32[]{:S(2)}) copy-start(f32[50,3072]{1,0:T(8,128)} %param.19) | copy-start | bytes 1843204
  7.2 223.4 %all-gather.4.cloned.1.call-start = ((), (), s32[]{:S(2)}) async-start(), calls=%async_computation | async-start | bytes 15728640 | tf_op jit(solution)/shard_map/all_gather | solution.py:131
  7.9 1.5 copy-start.11
  7.9 7.2 %copy-start.12 = (bf16[64,1536]{1,0:T(8,128)(2,1)S(1)}, bf16[64,1536]{1,0:T(8,128)(2,1)}, u32[]{:S(2)}) copy-start(bf16[64,1536]{1,0:T(8,128)(2,1)} %param.14) | copy-start | bytes 589828
  7.9 313.5 %all-gather.6.cloned.1.call-start = ((), (), s32[]{:S(2)}) async-start(), calls=%async_computation.1 | async-start | bytes 17694720 | tf_op jit(solution)/shard_map/all_gather | solution.py:100
  8.7 351.8 %all-gather.8.cloned.1.call-start = ((), (), s32[]{:S(2)}) async-start(), calls=%async_computation.2 | async-start | bytes 5898240 | tf_op jit(solution)/shard_map/all_gather | solution.py:101
  15.1 2.6 copy-start.13
  15.1 2.7 copy-start.14
  15.1 3.0 copy-start.10
  15.1 3.0 copy-start.15
  15.7 1.6 copy-start.1
  360.5 3.0 copy-start.2
  368.4 20.6 %collective-permute-start = (bf16[1,256,1536]{2,1,0:T(8,128)(2,1)S(1)}, bf16[1,256,1536]{2,1,0:T(8,128)(2,1)S(1)}, u32[]{:S(2)}, u32[]{:S(2)}) collective-permute-start(bf16[1,256,1536]{2,1,0:T(8,128)(2,1)S(1)} %bitcast.213), channel_id=1, source_target_pairs={{0,16},{1,17},{2,18},{3,19},{4,20},{5,21},{6,22},{7,23},{8,24},{9,... | collective-permute-start | bytes 2359304 | tf_op jit(solution)/shard_map/ppermute | solution.py:16
  380.6 11.8 %copy-start.3 = (f32[512,1536]{1,0:T(8,128)S(1)}, f32[512,1536]{1,0:T(8,128)}, u32[]{:S(2)}) copy-start(f32[512,1536]{1,0:T(8,128)} %copy-done.1) | copy-start | bytes 9437188
  407.6 6.3 %copy-start.9 = (bf16[1,256,1536]{2,1,0:T(8,128)(2,1)S(1)}, bf16[1,256,1536]{2,1,0:T(8,128)(2,1)}, u32[]{:S(2)}) copy-start(bf16[1,256,1536]{2,1,0:T(8,128)(2,1)} %get-tuple-element.43) | copy-start | bytes 2359300
  421.2 4.8 copy-start.4
  430.9 20.7 %collective-permute-start.1 = (bf16[1,256,1536]{2,1,0:T(8,128)(2,1)S(1)}, bf16[1,256,1536]{2,1,0:T(8,128)(2,1)S(1)}, u32[]{:S(2)}, u32[]{:S(2)}) collective-permute-start(bf16[1,256,1536]{2,1,0:T(8,128)(2,1)S(1)} %get-tuple-element.51), channel_id=1, source_target_pairs={{0,16},{1,17},{2,18},{3,19},{4,20},{5,21},{6,22},{7,23},{8,24},{9,... | collective-permute-start | bytes 2359304 | tf_op jit(solution)/shard_map/ppermute | solution.py:16
  444.5 7.1 %copy-start.5 = (f32[512,1536]{1,0:T(8,128)S(1)}, f32[512,1536]{1,0:T(8,128)}, u32[]{:S(2)}) copy-start(f32[512,1536]{1,0:T(8,128)} %copy-done.1) | copy-start | bytes 9437188
  483.6 4.8 copy-start.6
  493.9 4.7 copy-start.16
  496.0 6.5 %copy-start.7 = (bf16[1,2,1,256,3072]{4,3,1,2,0:T(8,128)(2,1)S(1)}, bf16[1,2,1,256,3072]{4,3,1,2,0:T(8,128)(2,1)}, u32[]{:S(2)}) copy-start(bf16[1,2,1,256,3072]{4,3,1,2,0:T(8,128)(2,1)} %copy.72) | copy-start | bytes 9437188
  501.3 5.8 %collective-permute-start.2 = (bf16[2,128,64]{1,2,0:T(8,128)(2,1)S(1)}, bf16[2,128,64]{1,2,0:T(8,128)(2,1)S(1)}, u32[]{:S(2)}, u32[]{:S(2)}) collective-permute-start(bf16[2,128,64]{1,2,0:T(8,128)(2,1)S(1)} %slice.225), channel_id=1, source_target_pairs={{16,0},{17,1},{18,2},{19,3},{20,4},{21,5},{22,6},{23,7},{24,8},{25... | collective-permute-start | bytes 98312 | tf_op jit(solution)/shard_map/ppermute | solution.py:16
  504.9 3.5 copy-start.8
Sparse Core Ops, SparseCore 0:
  9.6 220.9 all-gather.3
  232.1 89.2 all-gather.5
  323.0 37.4 all-gather.7
where the time goes:
time: 526 us; the launch traced here: 515 us
  waiting for transfers between devices  304 us (58%)
  local copies, waits for them, and re-layouts  86.1 us (16%)
  matrix products  65.1 us (12%)
  other arithmetic  30.9 us (6%)
  between operations  14.6 us (3%)
  starting transfers between devices  9.2 us (2%)
  blocking collectives  5.51 us (1%)
    all_gather x1, waiting for transfers between devices, body(): lax.all_gather(stale_cache, 'patch', axis=2, tiled=True)[0]  212 us
    all_gather x1, waiting for transfers between devices, body(): lax.all_gather(wqkv, 'fsdp', axis=1, tiled=True)  66.1 us
    unnamed x43, local copies, waits for them, and re-layouts  32.8 us
    dot_general x3, matrix products, project_in(): return jnp.dot(left, proj_full, preferred_element_type=jnp.float32)  22.8 us
    slice x3, local copies, waits for them, and re-layouts, attend_fn(): seen_rows[..., :model_width]  16 us
    dynamic_slice x1, local copies, waits for them, and re-layouts, body(): lax.dynamic_slice_in_dim(stale_all, first_video, group_size, 0)  16 us
    dot_general x3, matrix products, project_out(): return jnp.dot(left, out_full, preferred_element_type=jnp.float32)  15.3 us
    ppermute x3, waiting for transfers between devices, shifted(): return lax.ppermute(shard, axis, pairs)  13.7 us
  transfers between devices with their start and end apart: 6, of which 6 were waited for; matrix products, arithmetic and copies ran while one was open for 16% of the time, Pallas kernels for 0%

commit v1 on v0

--- a/solution.py
+++ b/solution.py
@@ -1,3 +1,4 @@
+import functools
 import math
 import jax
 import jax.numpy as jnp
@@ -8,6 +9,43 @@
 HD = 128
 TSTEPS = 50
 EPS = 1e-06
+
+
+def part_the_tracks(values, dim_k):
+    field_out = list(values.shape[1:])
+    field_out[dim_k] *= values.shape[0]
+    local_next = jnp.moveaxis(values, 0, dim_k).reshape(field_out)
+    return local_next
+
+
+def update_sections_on_mesh(obj, axis_key, pos_dim):
+    many = lax.axis_size(axis_key)
+    runs = []
+    h = 0
+    while h < many:
+        runs.append((h, (h + 1) % many))
+        h += 1
+    history = []
+    for jj, dev in runs:
+        history.append((dev, jj))
+    next_value, aux = ([], [])
+    it = 0
+    while it < many - 1:
+        if it % 2 == 0:
+            next_value.append(
+                lax.ppermute(next_value[-1] if next_value else obj, axis_name=axis_key, perm=runs)
+            )
+        else:
+            aux.append(lax.ppermute(aux[-1] if aux else obj, axis_key, perm=history))
+        it += 1
+    a_next = jnp.stack([*next_value[::-1], obj, *aux])
+    heard = lax.axis_index(axis_key) - len(next_value)
+    a_next = a_next[(jnp.arange(many) - heard) % many]
+    f_next = part_the_tracks(a_next, pos_dim)
+    return f_next
+
+
+part_signs = functools.partial(update_sections_on_mesh, axis_key="fsdp", pos_dim=1)
 
 
 def shifted(shard, axis, by):
@@ -96,10 +134,7 @@
     model_width = embed_weight.shape[1]
     patch_count = counts.shape[1]
     zero_index = jnp.zeros((), jnp.int32)
-    proj_full, out_full = (
-        lax.all_gather(wqkv, "fsdp", axis=1, tiled=True),
-        lax.all_gather(wo, "fsdp", axis=1, tiled=True),
-    )
+    proj_full, out_full = (part_signs(wqkv), lax.all_gather(wo, "fsdp", axis=1, tiled=True))
     proj_full = proj_full[0]
     out_full = out_full[0]
 

time: 526 us -> 427 us (0.81); the launches traced: 515 us -> 423 us
  waiting for transfers between devices: 304 us -> 175 us
  local copies, waits for them, and re-layouts: 86.1 us -> 105 us
  other arithmetic: 30.9 us -> 47.7 us
    all_gather x1, waiting for transfers between devices: 212 us -> 56.1 us  [body(): lax.all_gather(stale_cache, 'patch', axis=2, tiled=True)[0]]
    ppermute x0 -> x3, waiting for transfers between devices: none -> 103 us  [the longest x2 103 us: update_sections_on_mesh(): lax.ppermute(next_value[-1] if next_value else obj, axis_name=axis_key, p...]
    all_gather x1 -> x0, waiting for transfers between devices: 66.1 us -> none  [body(): lax.all_gather(wqkv, 'fsdp', axis=1, tiled=True)]
    gather x0 -> x3, local copies, waits for them, and re-layouts: none -> 19.2 us  [update_sections_on_mesh(): a_next = a_next[(jnp.arange(many) - heard) % many]]
    all_gather x1, waiting for transfers between devices: 10.2 us -> 0.85 us  [body(): lax.all_gather(wo, 'fsdp', axis=1, tiled=True)]
    unnamed x2 -> x3, other arithmetic: 1.34 us -> 8.8 us
    another operation x0 -> x1, other arithmetic: none -> 7.33 us  [update_sections_on_mesh(): a_next = jnp.stack([*next_value[::-1], obj, *aux])]
    unnamed x43 -> x61, local copies, waits for them, and re-layouts: 32.8 us -> 33.7 us
  transfers between devices with their start and end apart: 6 -> 8, of which waited for: 6 -> 7; matrix products, arithmetic and copies ran while one was open for 16% -> 26% of each run, Pallas kernels for 0% -> 0%
where the time goes in v1:
time: 427 us; the launch traced here: 423 us
  waiting for transfers between devices  175 us (41%)
  local copies, waits for them, and re-layouts  105 us (25%)
  matrix products  61.4 us (14%)
  other arithmetic  47.7 us (11%)
  between operations  14.9 us (3%)
  starting transfers between devices  14.3 us (3%)
  blocking collectives  4.61 us (1%)
    ppermute x2, waiting for transfers between devices, update_sections_on_mesh(): lax.ppermute(next_value[-1] if next_value else obj, axis_name=axis_key, p...  103 us
    all_gather x1, waiting for transfers between devices, body(): lax.all_gather(stale_cache, 'patch', axis=2, tiled=True)[0]  56.1 us
    unnamed x61, local copies, waits for them, and re-layouts  33.7 us
    gather x3, local copies, waits for them, and re-layouts, update_sections_on_mesh(): a_next = a_next[(jnp.arange(many) - heard) % many]  19.2 us
    dot_general x3, matrix products, project_in(): return jnp.dot(left, proj_full, preferred_element_type=jnp.float32)  18.9 us
    slice x3, local copies, waits for them, and re-layouts, attend_fn(): seen_rows[..., :model_width]  16 us
    dot_general x3, matrix products, project_out(): return jnp.dot(left, out_full, preferred_element_type=jnp.float32)  15.3 us
    dynamic_slice x1, local copies, waits for them, and re-layouts, body(): lax.dynamic_slice_in_dim(stale_all, first_video, group_size, 0)  14.4 us
  transfers between devices with their start and end apart: 8, of which 7 were waited for; matrix products, arithmetic and copies ran while one was open for 26% of the time, Pallas kernels for 0%

profile of v1, /device:TPU:0, one launch (start us, length us, event | category | flops | bytes accessed | tf_op | source)
XLA Modules:
  0.0 422.9 jit_solution(16945101103817618173)
XLA Ops:
  10.6 74.7 %collective-permute-done = bf16[1,384,4608]{2,1,0:T(8,128)(2,1)} collective-permute-done((bf16[1,384,4608]{2,1,0:T(8,128)(2,1)}, bf16[1,384,4608]{2,1,0:T(8,128)(2,1)}, u32[]{:S(2)}, u32[]{:S(2)}) %collective-permute-start) | collective-permute-done | bytes 3538976 | tf_op jit(solution)/shard_map/ppermute | solution.py:36
  85.2 2.5 collective-permute-start.1
  87.8 4.6 %all_gather.9 = bf16[2,1,256,64]{2,3,1,0:T(8,128)(2,1)S(1)} all-gather(bf16[2,1,128,64]{2,3,1,0:T(8,128)(2,1)S(1)} %convert_element_type.99), channel_id=1, replica_groups=mesh['section'=2,'patch'=4,'fsdp'=4] {'section'}, dimensions={2}, use_global_device_ids=true | all-gather | bytes 98304 | tf_op jit(solution)/shard_map/all_gather | solution.py:147
  97.9 28.5 %collective-permute-done.1 = bf16[1,384,4608]{2,1,0:T(8,128)(2,1)} collective-permute-done((bf16[1,384,4608]{2,1,0:T(8,128)(2,1)}, bf16[1,384,4608]{2,1,0:T(8,128)(2,1)}, u32[]{:S(2)}, u32[]{:S(2)}) %collective-permute-start.1) | collective-permute-done | bytes 3538976 | tf_op jit(solution)/shard_map/ppermute | solution.py:36
  126.5 7.3 %pad_maximum_fusion = bf16[4,1,384,4608]{3,2,1,0:T(8,128)(2,1)S(1)} fusion(bf16[1,1,384,4608]{3,2,1,0:T(8,128)(2,1)} %bitcast.4, bf16[1,1,384,4608]{3,2,1,0:T(8,128)(2,1)S(1)} %bitcast.205, bf16[1,1,384,4608]{3,2,1,0:T(8,128)(2,1)} %bitcast.2, bf16[1,1,384,4608]{3,2,1,0:T(8,128)(2,1)} %bitcast.1), kind=kLoop, calls=%fused_computation.2 | loop fusion | flops 21233664 | bytes 28311552 | tf_op jit(solution)/shard_map/stack | solution.py:41
  133.8 5.3 %slice_bitcast_fusion.1 = (bf16[4,384,2304]{2,1,0:T(8,128)(2,1)}, bf16[4,384,2304]{2,1,0:T(8,128)(2,1)}) fusion(bf16[4,1,384,4608]{3,2,1,0:T(8,128)(2,1)S(1)} %pad_maximum_fusion), kind=kLoop, calls=%fused_computation.20 | loop fusion | bytes 28311552 | tf_op jit(solution)/shard_map/gather | solution.py:43
  139.1 7.0 %gather_fusion = bf16[4,384,2304]{2,1,0:T(8,128)(2,1)} fusion(bf16[4,384,2304]{2,1,0:T(8,128)(2,1)} %get-tuple-element.32, s32[1024]{0:T(1024)S(1)} %pad_clamp_fusion), kind=kCustom, calls=%fused_computation | custom fusion | bytes 14155792 | tf_op jit(solution)/shard_map/gather | solution.py:43
  146.1 6.9 %gather_fusion.1 = bf16[4,384,2304]{2,1,0:T(8,128)(2,1)} fusion(bf16[4,384,2304]{2,1,0:T(8,128)(2,1)} %get-tuple-element.33, s32[1024]{0:T(1024)S(1)} %pad_clamp_fusion), kind=kCustom, calls=%fused_computation.1 | custom fusion | bytes 14155792 | tf_op jit(solution)/shard_map/gather | solution.py:43
  153.0 7.5 %pad_maximum_fusion.1 = bf16[4,1,384,4608]{3,2,0,1:T(8,128)(2,1)S(1)} fusion(bf16[4,1,384,2304]{3,2,0,1:T(8,128)(2,1)} %bitcast.197, bf16[4,1,384,2304]{3,2,0,1:T(8,128)(2,1)} %bitcast.196), kind=kLoop, calls=%fused_computation.3 | loop fusion | flops 28311552 | bytes 28311552
  160.5 3.9 convolution_bitcast_fusion.2
  169.1 2.3 select_dynamic-update-slice_fusion.1
  174.5 56.1 %all-gather.3.cloned.1.call-done = bf16[1,2,4,256,3072]{4,3,2,1,0:T(8,128)(2,1)} async-done(((bf16[1,2,1,256,3072]{4,3,2,1,0:T(8,128)(2,1)}), bf16[1,2,4,256,3072]{4,3,2,1,0:T(8,128)(2,1)}) %all-gather.3.cloned.1.call-update) | async-done | bytes 12582928 | tf_op jit(solution)/shard_map/all_gather | solution.py:166
  230.6 14.4 %constant_dynamic-slice_fusion.3 = (bf16[1,1024,3072]{2,1,0:T(8,128)(2,1)}, bf16[1,1024,3072]{2,1,0:T(8,128)(2,1)}, bf16[1,1024,3072]{2,1,0:T(8,128)(2,1)}) fusion(bf16[2,1024,3072]{2,1,0:T(8,128)(2,1)} %bitcast.198, s32[]{:T(128)S(6)} %min.12, s32[]{:T(128)S(6)} %min.11, s32[]{:T(128)S(6)} %min.10), kind=kLoop, calls=%fused_computation.146 | loop fusion | bytes 37748748 | tf_op jit(solution)/shard_map/dynamic_slice | solution.py:182
  245.0 8.6 %copy.54 = bf16[1,1024,3072]{1,2,0:T(8,128)(2,1)} copy(bf16[1,1024,3072]{2,1,0:T(8,128)(2,1)} %get-tuple-element.36) | data formatting | bytes 12582912
  254.9 3.6 fusion.121
  258.4 2.0 fusion
  260.5 3.0 fusion.3
  263.5 3.4 fusion.65
  267.8 2.0 broadcast_in_dim.85
  270.9 4.9 %bitcast_dynamic-update-slice_fusion.1 = (f32[2,256,1536]{2,1,0:T(8,128)}, bf16[256,1536]{1,0:T(8,128)(2,1)S(1)}) fusion(f32[2,256,1536]{2,1,0:T(8,128)} %broadcast_in_dim.85, s32[]{:T(128)S(6)} %min.10, pred[]{:T(512)S(6)} %eq.29, bf16[256,1536]{0,1:T(8,128)(2,1)S(1)} %bitcast.223, bf16[1,1536,1536]{2,1,0:T(8,128)(2,1)} %all-gather.5.cloned.1.call-done, ...), kind=kOutput, calls=%fused_computation.72 | convolution fusion | flops 1209925632 | bytes 9443333 | tf_op jit(solution)/shard_map/dot_general | solution.py:145
  275.8 3.4 collective-permute-start.3
  279.2 8.6 %copy.55 = bf16[1,1024,3072]{1,2,0:T(8,128)(2,1)} copy(bf16[1,1024,3072]{2,1,0:T(8,128)(2,1)} %get-tuple-element.35) | data formatting | bytes 12582912
  287.8 8.5 %collective-permute-done.3 = bf16[1,256,1536]{2,1,0:T(8,128)(2,1)S(1)} collective-permute-done((bf16[1,256,1536]{2,1,0:T(8,128)(2,1)S(1)}, bf16[1,256,1536]{2,1,0:T(8,128)(2,1)S(1)}, u32[]{:S(2)}, u32[]{:S(2)}) %collective-permute-start.3) | collective-permute-done | bytes 786464 | tf_op jit(solution)/shard_map/ppermute | solution.py:54
  299.8 7.5 %convolution_bitcast_fusion.1 = f32[1,256,4608]{2,1,0:T(8,128)S(1)} fusion(bf16[1536,4608]{1,0:T(8,128)(2,1)} %bitcast.200, f32[1536]{0:T(1024)S(1)} %get-tuple-element.22, f32[1536]{0:T(1024)S(1)} %get-tuple-element.17, f32[256]{0:T(256)S(1)} %add_rsqrt_fusion.6, f32[256]{0:T(256)S(1)} %broadcast_multiply_fusion.2, ...), kind=kOutput, calls=%fused_computation.22 | convolution fusion | flops 3626631168 | bytes 21252096 | tf_op jit(solution)/shard_map/dot_general | solution.py:142
  312.2 2.7 constant_dynamic-update-slice_fusion.2
  314.9 6.3 %fusion.120 = (bf16[1,1024,1536]{1,2,0:T(8,128)(2,1)}, bf16[1,1024,1536]{1,2,0:T(8,128)(2,1)}) fusion(bf16[1,1024,3072]{1,2,0:T(8,128)(2,1)} %constant_dynamic-update-slice_fusion.2), kind=kLoop, calls=%fused_computation.197 | loop fusion | bytes 12582912 | tf_op jit(solution)/shard_map/slice | solution.py:190
  321.4 3.9 fusion.1
  325.4 3.0 fusion.5
  328.4 4.7 %fusion.64 = bf16[1,256,12,128]{1,3,2,0:T(8,128)(2,1)S(1)} fusion(bf16[1024,12,128]{0,2,1:T(8,128)(2,1)} %bitcast.211, f32[12,256,1024]{2,1,0:T(8,128)S(1)} %get-tuple-element.60, f32[12,256]{1,0:T(8,128)S(1)} %get-tuple-element.59, pred[1024]{0:T(1024)(128)(4,1)S(1)} %get-tuple-element.27, f32[256,12]{0,1:T(8,128)S(1)} %bitcast.219), kind=kOutput, calls=%fused_computation.69 | convolution fusion | flops 818675712 | bytes 16540672 | tf_op jit(solution)/shard_map/ghqk,gkhd->gqhd/dot_general | solution.py:87
  333.2 4.9 %fusion.122 = (bf16[1,256,1536]{2,1,0:T(8,128)(2,1)S(1)}, f32[2,256,1536]{2,1,0:T(8,128)}) fusion(f32[2,256,1536]{2,1,0:T(8,128)} %get-tuple-element.61, s32[]{:T(128)S(6)} %min.11, bf16[256,1536]{0,1:T(8,128)(2,1)S(1)} %bitcast.214, bf16[1,1536,1536]{2,1,0:T(8,128)(2,1)} %all-gather.5.cloned.1.call-done, f32[1536]{0:T(1024)S(1)} %get-tuple-element.18, ...), kind=kOutput, calls=%fused_computation.199 | convolution fusion | flops 1209925632 | bytes 10229765 | tf_op jit(solution)/shard_map/dot_general | solution.py:145
  338.1 4.5 %collective-permute-start.4 = (bf16[1,256,1536]{2,1,0:T(8,128)(2,1)S(1)}, bf16[1,256,1536]{2,1,0:T(8,128)(2,1)S(1)}, u32[]{:S(2)}, u32[]{:S(2)}) collective-permute-start(bf16[1,256,1536]{2,1,0:T(8,128)(2,1)S(1)} %get-tuple-element.53), channel_id=1, source_target_pairs={{0,16},{1,17},{2,18},{3,19},{4,20},{5,21},{6,22},{7,23},{8,24},{9,... | collective-permute-start | bytes 2359304 | tf_op jit(solution)/shard_map/ppermute | solution.py:54
  343.0 8.8 %copy.56 = bf16[1,1024,3072]{1,2,0:T(8,128)(2,1)} copy(bf16[1,1024,3072]{2,1,0:T(8,128)(2,1)} %get-tuple-element.34) | data formatting | bytes 12582912
  351.9 3.9 copy.72
  355.8 3.2 collective-permute-done.4
  359.6 7.5 %convolution_bitcast_fusion = f32[1,256,4608]{2,1,0:T(8,128)S(1)} fusion(bf16[1536,4608]{1,0:T(8,128)(2,1)} %bitcast.201, f32[1536]{0:T(1024)S(1)} %get-tuple-element.21, f32[1536]{0:T(1024)S(1)} %get-tuple-element.16, f32[256]{0:T(256)S(1)} %add_rsqrt_fusion.3, f32[256]{0:T(256)S(1)} %broadcast_multiply_fusion.1, ...), kind=kOutput, calls=%fused_computation.21 | convolution fusion | flops 3626631168 | bytes 21252096 | tf_op jit(solution)/shard_map/dot_general | solution.py:142
  370.0 2.6 copy.37
  372.6 2.7 constant_dynamic-update-slice_fusion
  375.3 6.2 %fusion.119 = (bf16[1,1024,1536]{1,2,0:T(8,128)(2,1)}, bf16[1,1024,1536]{1,2,0:T(8,128)(2,1)}) fusion(bf16[1,1024,3072]{1,2,0:T(8,128)(2,1)} %constant_dynamic-update-slice_fusion), kind=kLoop, calls=%fused_computation.196 | loop fusion | bytes 12582912 | tf_op jit(solution)/shard_map/slice | solution.py:190
  381.5 2.3 copy.38
  383.8 4.2 fusion.2
  388.0 3.0 fusion.7
  391.0 4.7 %fusion.63 = bf16[1,256,12,128]{1,3,2,0:T(8,128)(2,1)S(1)} fusion(bf16[1024,12,128]{0,2,1:T(8,128)(2,1)} %bitcast.210, f32[12,256,1024]{2,1,0:T(8,128)S(1)} %get-tuple-element.64, f32[12,256]{1,0:T(8,128)S(1)} %get-tuple-element.63, pred[1024]{0:T(1024)(128)(4,1)S(1)} %copy-done.19, f32[256,12]{0,1:T(8,128)S(1)} %bitcast.220), kind=kOutput, calls=%fused_computation.67 | convolution fusion | flops 818675712 | bytes 16540672 | tf_op jit(solution)/shard_map/ghqk,gkhd->gqhd/dot_general | solution.py:87
  395.8 5.5 %fusion.57 = f32[2,256,1536]{2,1,0:T(8,128)} fusion(f32[2,256,1536]{2,1,0:T(8,128)} %get-tuple-element.54, s32[]{:T(128)S(6)} %min.12, bf16[256,1536]{0,1:T(8,128)(2,1)S(1)} %bitcast.213, bf16[1,1536,1536]{2,1,0:T(8,128)(2,1)} %all-gather.5.cloned.1.call-done, f32[1536]{0:T(1024)S(1)} %copy-done.17, pred[]{:T(512)S(6)} %select_n.205, ...), kind=kOutput, calls=%fused_computation.55 | convolution fusion | flops 1209925632 | bytes 11016198 | tf_op jit(solution)/shard_map/dot_general | solution.py:145
  401.3 2.2 reduce_sum.187
  403.5 2.5 multiply_reduce_fusion
  406.0 2.7 fusion.73
  410.0 2.3 bitcast_dynamic-update-slice_fusion
  412.3 2.2 collective-permute-done.5
  (122 shorter events, 34.8 us)
Async XLA Ops:
  7.2 335.5 %copy-start = (f32[50,3072]{1,0:T(8,128)S(1)}, f32[50,3072]{1,0:T(8,128)}, u32[]{:S(2)}) copy-start(f32[50,3072]{1,0:T(8,128)} %param.19) | copy-start | bytes 1843204
  7.2 80.6 %copy-start.14 = (f32[2,1,128,64]{2,3,1,0:T(8,128)S(1)}, f32[2,1,128,64]{2,3,1,0:T(8,128)}, u32[]{:S(2)}) copy-start(f32[2,1,128,64]{2,3,1,0:T(8,128)} %param.11) | copy-start | bytes 196612
  7.2 85.3 %copy-start.22 = (s32[2,4]{1,0:T(2,128)S(1)}, s32[2,4]{1,0:T(2,128)}, u32[]{:S(2)}) copy-start(s32[2,4]{1,0:T(2,128)} %param.12) | copy-start | bytes 100
  7.2 86.8 %copy-start.23 = (s32[2]{0:T(128)S(1)}, s32[2]{0:T(128)}, u32[]{:S(2)}) copy-start(s32[2]{0:T(128)} %param.13) | copy-start | bytes 28
  7.2 86.8 %copy-start.13 = (f32[1,50,4608]{2,0,1:T(1,128)S(1)}, f32[1,50,4608]{2,0,1:T(1,128)}, u32[]{:S(2)}) copy-start(f32[1,50,4608]{2,0,1:T(1,128)} %param.18) | copy-start | bytes 2764804
  7.2 88.1 %copy-start.18 = (f32[1,3072]{1,0:T(1,128)S(1)}, f32[1,3072]{1,0:T(1,128)}, u32[]{:S(2)}) copy-start(f32[1,3072]{1,0:T(1,128)} %param.17) | copy-start | bytes 36868
  7.2 88.1 %copy-start.16 = (bf16[64,1536]{1,0:T(8,128)(2,1)S(1)}, bf16[64,1536]{1,0:T(8,128)(2,1)}, u32[]{:S(2)}) copy-start(bf16[64,1536]{1,0:T(8,128)(2,1)} %param.14) | copy-start | bytes 589828
  7.2 223.3 %all-gather.3.cloned.1.call-start = ((), (), s32[]{:S(2)}) async-start(), calls=%async_computation | async-start | bytes 15728640 | tf_op jit(solution)/shard_map/all_gather | solution.py:166
  8.0 259.9 %all-gather.5.cloned.1.call-start = ((), (), s32[]{:S(2)}) async-start(), calls=%async_computation.1 | async-start | bytes 5898240 | tf_op jit(solution)/shard_map/all_gather | solution.py:137
  8.0 77.2 %collective-permute-start = (bf16[1,384,4608]{2,1,0:T(8,128)(2,1)}, bf16[1,384,4608]{2,1,0:T(8,128)(2,1)}, u32[]{:S(2)}, u32[]{:S(2)}) collective-permute-start(bf16[1,384,4608]{2,1,0:T(8,128)(2,1)} %param.15), channel_id=1, source_target_pairs={{0,1},{1,2},{2,3},{3,0},{4,5},{5,6},{6,7},{7,4},{8,9},{9,10},{10,1... | collective-permute-start | bytes 10616840 | tf_op jit(solution)/shard_map/ppermute | solution.py:36
  8.5 89.4 %collective-permute-start.2 = (bf16[1,384,4608]{2,1,0:T(8,128)(2,1)}, bf16[1,384,4608]{2,1,0:T(8,128)(2,1)}, u32[]{:S(2)}, u32[]{:S(2)}) collective-permute-start(bf16[1,384,4608]{2,1,0:T(8,128)(2,1)} %param.15), channel_id=1, source_target_pairs={{1,0},{2,1},{3,2},{0,3},{5,4},{6,5},{7,6},{4,7},{9,8},{10,9},{11,1... | collective-permute-start | bytes 10616840 | tf_op jit(solution)/shard_map/ppermute | solution.py:39
  85.2 41.2 %collective-permute-start.1 = (bf16[1,384,4608]{2,1,0:T(8,128)(2,1)}, bf16[1,384,4608]{2,1,0:T(8,128)(2,1)}, u32[]{:S(2)}, u32[]{:S(2)}) collective-permute-start(bf16[1,384,4608]{2,1,0:T(8,128)(2,1)} %collective-permute-done), channel_id=1, source_target_pairs={{0,1},{1,2},{2,3},{3,0},{4,5},{5,6},{6,7},{7,4},{8,9},{9,10},{10,1... | collective-permute-start | bytes 10616840 | tf_op jit(solution)/shard_map/ppermute | solution.py:36
  92.8 0.6 copy-start.20
  95.3 31.1 %copy-start.9 = (bf16[1,384,4608]{2,1,0:T(8,128)(2,1)S(1)}, bf16[1,384,4608]{2,1,0:T(8,128)(2,1)}, u32[]{:S(2)}) copy-start(bf16[1,384,4608]{2,1,0:T(8,128)(2,1)} %param.15) | copy-start | bytes 10616836
  95.9 1.6 copy-start.1
  153.0 7.5 %copy-start.2 = (f32[512,1536]{1,0:T(8,128)S(1)}, f32[512,1536]{1,0:T(8,128)}, u32[]{:S(2)}) copy-start(f32[512,1536]{1,0:T(8,128)} %copy-done.1) | copy-start | bytes 9437188
  160.5 5.1 %copy-start.8 = (bf16[4,1,384,4608]{3,2,0,1:T(8,128)(2,1)}, bf16[4,1,384,4608]{3,2,0,1:T(8,128)(2,1)S(1)}, u32[]{:S(2)}) copy-start(bf16[4,1,384,4608]{3,2,0,1:T(8,128)(2,1)S(1)} %pad_maximum_fusion.1) | copy-start | bytes 42467332
  267.8 3.0 copy-start.3
  275.8 20.6 %collective-permute-start.3 = (bf16[1,256,1536]{2,1,0:T(8,128)(2,1)S(1)}, bf16[1,256,1536]{2,1,0:T(8,128)(2,1)S(1)}, u32[]{:S(2)}, u32[]{:S(2)}) collective-permute-start(bf16[1,256,1536]{2,1,0:T(8,128)(2,1)S(1)} %bitcast.222), channel_id=1, source_target_pairs={{0,16},{1,17},{2,18},{3,19},{4,20},{5,21},{6,22},{7,23},{8,24},{9,... | collective-permute-start | bytes 2359304 | tf_op jit(solution)/shard_map/ppermute | solution.py:54
  287.8 11.9 %copy-start.4 = (f32[512,1536]{1,0:T(8,128)S(1)}, f32[512,1536]{1,0:T(8,128)}, u32[]{:S(2)}) copy-start(f32[512,1536]{1,0:T(8,128)} %copy-done.1) | copy-start | bytes 9437188
  314.9 6.3 %copy-start.12 = (bf16[1,256,1536]{2,1,0:T(8,128)(2,1)S(1)}, bf16[1,256,1536]{2,1,0:T(8,128)(2,1)}, u32[]{:S(2)}) copy-start(bf16[1,256,1536]{2,1,0:T(8,128)(2,1)} %get-tuple-element.45) | copy-start | bytes 2359300
  328.4 4.8 %copy-start.5 = (f32[512,1536]{1,0:T(8,128)S(1)}, f32[512,1536]{1,0:T(8,128)}, u32[]{:S(2)}) copy-start(f32[512,1536]{1,0:T(8,128)} %copy-done.1) | copy-start | bytes 9437188
  338.1 20.8 %collective-permute-start.4 = (bf16[1,256,1536]{2,1,0:T(8,128)(2,1)S(1)}, bf16[1,256,1536]{2,1,0:T(8,128)(2,1)S(1)}, u32[]{:S(2)}, u32[]{:S(2)}) collective-permute-start(bf16[1,256,1536]{2,1,0:T(8,128)(2,1)S(1)} %get-tuple-element.53), channel_id=1, source_target_pairs={{0,16},{1,17},{2,18},{3,19},{4,20},{5,21},{6,22},{7,23},{8,24},{9,... | collective-permute-start | bytes 2359304 | tf_op jit(solution)/shard_map/ppermute | solution.py:54
  351.9 7.1 %copy-start.6 = (f32[512,1536]{1,0:T(8,128)S(1)}, f32[512,1536]{1,0:T(8,128)}, u32[]{:S(2)}) copy-start(f32[512,1536]{1,0:T(8,128)} %copy-done.1) | copy-start | bytes 9437188
  375.3 8.5 %copy-start.19 = (pred[1024]{0:T(1024)(128)(4,1)S(1)}, pred[1024]{0:T(1024)(128)(4,1)}, u32[]{:S(2)}) copy-start(pred[1024]{0:T(1024)(128)(4,1)} %get-tuple-element.26) | copy-start | bytes 3076
  391.0 4.8 %copy-start.7 = (f32[512,1536]{1,0:T(8,128)S(1)}, f32[512,1536]{1,0:T(8,128)}, u32[]{:S(2)}) copy-start(f32[512,1536]{1,0:T(8,128)} %copy-done.1) | copy-start | bytes 9437188
  391.0 4.8 %copy-start.17 = (f32[1536]{0:T(1024)S(1)}, f32[1536]{0:T(1024)}, u32[]{:S(2)}) copy-start(f32[1536]{0:T(1024)} %get-tuple-element.15) | copy-start | bytes 18436
  401.3 4.7 %copy-start.21 = (pred[2,256]{1,0:T(4,128)(4,1)S(1)}, pred[2,256]{1,0:T(4,128)(4,1)}, u32[]{:S(2)}) copy-start(pred[2,256]{1,0:T(4,128)(4,1)} %copy-done.20) | copy-start | bytes 1540
  401.3 4.7 %copy-start.25 = (bf16[1536,64]{0,1:T(8,128)(2,1)S(1)}, bf16[1536,64]{0,1:T(8,128)(2,1)}, u32[]{:S(2)}) copy-start(bf16[1536,64]{0,1:T(8,128)(2,1)} %param.20) | copy-start | bytes 589828
  403.4 6.5 %copy-start.10 = (bf16[1,2,1,256,3072]{4,3,1,2,0:T(8,128)(2,1)S(1)}, bf16[1,2,1,256,3072]{4,3,1,2,0:T(8,128)(2,1)}, u32[]{:S(2)}) copy-start(bf16[1,2,1,256,3072]{4,3,1,2,0:T(8,128)(2,1)} %copy.72) | copy-start | bytes 9437188
  403.5 6.5 %copy-start.24 = (pred[256]{0:T(512)(128)(4,1)S(1)}, pred[256]{0:T(512)(128)(4,1)}, u32[]{:S(2)}) copy-start(pred[256]{0:T(512)(128)(4,1)} %get-tuple-element.29) | copy-start | bytes 772
  408.7 6.5 %copy-start.15 = (f32[2,1,128,64]{2,3,1,0:T(8,128)S(1)}, f32[2,1,128,64]{2,3,1,0:T(8,128)}, u32[]{:S(2)}) copy-start(f32[2,1,128,64]{2,3,1,0:T(8,128)} %param.11) | copy-start | bytes 196612
  408.7 5.8 %collective-permute-start.5 = (bf16[2,128,64]{1,2,0:T(8,128)(2,1)S(1)}, bf16[2,128,64]{1,2,0:T(8,128)(2,1)S(1)}, u32[]{:S(2)}, u32[]{:S(2)}) collective-permute-start(bf16[2,128,64]{1,2,0:T(8,128)(2,1)S(1)} %slice.229), channel_id=1, source_target_pairs={{16,0},{17,1},{18,2},{19,3},{20,4},{21,5},{22,6},{23,7},{24,8},{25... | collective-permute-start | bytes 98312 | tf_op jit(solution)/shard_map/ppermute | solution.py:54
  412.3 3.5 copy-start.11
Sparse Core Ops, SparseCore 0:
  9.6 220.8 all-gather.2
  232.1 35.6 all-gather.4
